TPU v7x, 512 devices: a whole 4x4x16 slice. The times are simulated.
512 devices in a mesh: frm: 32 (over z, core), col: 16 (over x, y).
Axes of the slice: x: 4, y: 4, z: 16, core: 2. Of those that a mesh axis runs over, the one named last changes fastest.
Arguments:
- video: bfloat16 [64, 32, 512, 512], P('frm', None, 'col'), may hold values from -6 to 6
- norm_gain: float32 [512], replicated, may hold values from 0.25 to 1.75
- w_query: bfloat16 [512, 512], replicated, may hold values from -1 to 1
- w_key: bfloat16 [512, 512], replicated, may hold values from -1 to 1
- w_value: bfloat16 [512, 512], replicated, may hold values from -0.25 to 0.25
- w_out: bfloat16 [512, 512], replicated, may hold values from -0.25 to 0.25
- w_time: bfloat16 [3, 512, 512], replicated, may hold values from -0.15625 to 0.15625
- w_depth: float32 [3, 3, 512], replicated, may hold values from -2 to 2
Outputs:
- encoded: bfloat16 [32, 32, 512, 512], P('frm', None, 'col')
All inputs are finite; a program needn't handle non-finite values.
Results may differ from a plain program's by a relative error of at most 0.012.
The roundings to bfloat16 on the way count: a program that leaves them out, or rounds other values in their place, can miss the bound.
Values may be sent and summed in bfloat16 or wider, within the bound.
A program may use at most 64 MiB of HBM per device.

v0:
```python
import math

import jax
import jax.numpy as jnp
from jax import lax
from jax.sharding import PartitionSpec as P

FRAMES = 64
VIDEOS = 1


epsilon = 1e-06


def from_behind(value, axis, steps):
    count = lax.axis_size(axis)
    initial, last = (max(0, -steps), min(count, count - steps))
    return lax.ppermute(value, axis, [(source, source + steps) for source in range(initial, last)])


def padded_2(block, sides, width):
    for axis, dim in sides:
        count = lax.axis_size(axis)
        forward = [(i, i + 1) for i in range(count - 1)]
        backward = [(target, source) for source, target in forward]
        low = lax.ppermute(
            lax.slice_in_dim(block, block.shape[dim] - width, None, axis=dim), axis, forward
        )
        high = lax.ppermute(lax.slice_in_dim(block, 0, width, axis=dim), axis, backward)
        block = jnp.concatenate([low, block, high], axis=dim)
    return block


def attend_block(block_in, norm_gain, w_query, w_key, w_value, w_out):
    channels = block_in.shape[-1]
    widened = block_in.reshape(-1, channels).astype(jnp.float32)
    normed = (
        widened
        * lax.rsqrt(jnp.mean(widened * widened, axis=-1, keepdims=True) + epsilon)
        * norm_gain
    ).astype(jnp.bfloat16)
    grid_shape = (VIDEOS, FRAMES, -1, channels)
    queries = (
        jnp.dot(normed, w_query, preferred_element_type=jnp.float32)
        .astype(jnp.bfloat16)
        .reshape(grid_shape)
    )
    key_proj = (
        jnp.dot(normed, w_key, preferred_element_type=jnp.float32)
        .astype(jnp.bfloat16)
        .reshape(grid_shape)
    )
    values = (
        jnp.dot(normed, w_value, preferred_element_type=jnp.float32)
        .astype(jnp.bfloat16)
        .reshape(grid_shape)
    )
    scores = jnp.einsum(
        "bqpc,bkpc->bpqk", queries, key_proj, preferred_element_type=jnp.float32
    ) / math.sqrt(channels)
    causal = jnp.arange(FRAMES)[:, None] >= jnp.arange(FRAMES)[None, :]
    scores = jnp.where(causal, scores, -1e30)
    raised = jnp.exp(scores - jnp.max(scores, axis=-1, keepdims=True))
    weights = (raised / jnp.sum(raised, axis=-1, keepdims=True)).astype(jnp.bfloat16)
    attended = jnp.einsum(
        "bpqk,bkpc->bqpc", weights, values, preferred_element_type=jnp.float32
    ).astype(jnp.bfloat16)
    projected = jnp.dot(attended.reshape(-1, channels), w_out, preferred_element_type=jnp.float32)
    return (widened + projected).astype(jnp.bfloat16).reshape(block_in.shape)


def time_conv(prior_frames, even_frames, odd_frames, w_time):
    channels = even_frames.shape[-1]
    summed = jnp.dot(
        prior_frames.reshape(-1, channels), w_time[0], preferred_element_type=jnp.float32
    )
    summed = summed + jnp.dot(
        even_frames.reshape(-1, channels), w_time[1], preferred_element_type=jnp.float32
    )
    summed = summed + jnp.dot(
        odd_frames.reshape(-1, channels), w_time[2], preferred_element_type=jnp.float32
    )
    return jax.nn.silu(summed).astype(jnp.bfloat16).reshape(even_frames.shape)


def local(video, norm_gain, w_query, w_key, w_value, w_out, w_time, w_depth):
    mixed_rows = attend_block(
        lax.all_to_all(video, "frm", split_axis=1, concat_axis=0, tiled=True),
        norm_gain,
        w_query,
        w_key,
        w_value,
        w_out,
    )
    returned = lax.all_to_all(mixed_rows, "frm", split_axis=0, concat_axis=1, tiled=True)
    prior_frame = from_behind(returned[-1:], "frm", 1)
    even_frames = returned[0::2]
    odd_frames = returned[1::2]
    prior_frames = jnp.concatenate([prior_frame, odd_frames[:-1]], axis=0)
    first_index = lax.axis_index("frm") * returned.shape[0] + 2 * jnp.arange(
        even_frames.shape[0], dtype=jnp.int32
    )
    starts = first_index % FRAMES == 0
    prior_frames = jnp.where(starts[:, None, None, None], even_frames, prior_frames)
    activated = time_conv(prior_frames, even_frames, odd_frames, w_time)
    rimmed = padded_2(activated, (("col", 2),), 1)
    rows = activated.shape[1]
    cols = activated.shape[2]
    padded = jnp.pad(rimmed.astype(jnp.float32), ((0, 0), (1, 1), (0, 0), (0, 0)))
    summed = jnp.zeros(activated.shape, jnp.float32)
    for row_step in range(3):
        for col_step in range(3):
            summed = (
                summed
                + padded[:, row_step : row_step + rows, col_step : col_step + cols]
                * w_depth[row_step, col_step]
            )
    return summed.astype(jnp.bfloat16)


def solution(mesh):
    return jax.shard_map(
        local,
        mesh=mesh,
        in_specs=(P("frm", None, "col", None), P(), P(), P(), P(), P(), P(), P()),
        out_specs=P("frm", None, "col", None),
        check_vma=False,
    )
```

profile of v0, /device:TPU:1, one launch (start us, length us, event | category | flops | bytes accessed | tf_op | source)
XLA Modules:
  0.0 274.3 jit_solution(11192743472726212469)
XLA Ops:
  0.0 3.2 %copy.22 = bf16[2,32,32,512]{3,2,0,1:T(8,128)(2,1)} copy(bf16[2,32,32,512]{3,2,1,0:T(8,128)(2,1)} %param.8) | data formatting | bytes 4194304 | tf_op args[0]
  3.2 16.7 %all-to-all-start = ((bf16[2,32,32,512]{3,2,0,1:T(8,128)(2,1)}), bf16[2,32,32,512]{3,2,0,1:T(8,128)(2,1)S(1)}, u32[]{:S(2)}, u32[]{:S(2)}) async-start(bf16[2,32,32,512]{3,2,0,1:T(8,128)(2,1)} %copy.22), calls=%async_computation | async-start | bytes 4194304 | tf_op jit(solution)/shard_map/all_to_all | solution.py:88
  20.0 98.3 %all-to-all-done = bf16[2,32,32,512]{3,2,0,1:T(8,128)(2,1)S(1)} async-done(((bf16[2,32,32,512]{3,2,0,1:T(8,128)(2,1)}), bf16[2,32,32,512]{3,2,0,1:T(8,128)(2,1)S(1)}, u32[]{:S(2)}, u32[]{:S(2)}) %all-to-all-start) | async-done | bytes 2097184 | tf_op jit(solution)/shard_map/all_to_all | solution.py:88
  118.9 0.5 fusion.3
  119.5 1.3 convolution_convert_fusion
  120.8 1.3 convolution_convert_fusion.1
  122.1 2.4 fusion.34
  124.8 2.6 convolution_convert_fusion.2
  127.4 6.4 %convert_bitcast_fusion = bf16[1,64,32,512]{3,1,2,0:T(8,128)(2,1)} fusion(bf16[64,32,512]{2,1,0:T(8,128)(2,1)} %bitcast.91, f32[32,64]{1,0:T(8,128)S(1)} %fusion.54, f32[32,64,64]{1,2,0:T(8,128)} %copy-done.8), kind=kOutput, calls=%fused_computation.41 | convolution fusion | flops 135661632 | bytes 4726784 | tf_op jit(solution)/shard_map/bpqk,bkpc->bqpc/dot_general | solution.py:65
  133.8 2.8 %copy.29 = bf16[1,64,32,512]{3,2,1,0:T(8,128)(2,1)S(1)} copy(bf16[1,64,32,512]{3,1,2,0:T(8,128)(2,1)} %convert_bitcast_fusion) | data formatting | bytes 4194304 | tf_op jit(solution)/shard_map/convert_element_type | solution.py:67
  136.6 1.3 fusion.4
  137.9 105.9 %all_to_all.24 = bf16[64,1,32,512]{3,2,1,0:T(8,128)(2,1)S(1)} all-to-all(bf16[64,1,32,512]{3,2,1,0:T(8,128)(2,1)S(1)} %bitcast.78), channel_id=1, replica_groups=mesh['frm'=32,'col'=16] {'frm'}, dimensions={0} | all-to-all | bytes 4194304 | tf_op jit(solution)/shard_map/all_to_all | solution.py:95
  243.7 2.0 slice_bitcast_fusion
  245.8 2.0 collective-permute-start
  247.8 2.2 fusion.39
  250.0 0.7 fusion.41
  250.7 9.1 %collective-permute-done = bf16[1,32,32,512]{3,2,1,0:T(8,128)(2,1)} collective-permute-done((bf16[1,32,32,512]{3,2,1,0:T(8,128)(2,1)}, bf16[1,32,32,512]{3,2,1,0:T(8,128)(2,1)}, u32[]{:S(2)}, u32[]{:S(2)}) %collective-permute-start) | collective-permute-done | bytes 1048608 | tf_op jit(solution)/shard_map/ppermute | solution.py:18
  259.8 1.3 bitcast_select_fusion
  261.1 1.1 multiply_convert_fusion
  262.3 3.2 %collective-permute-start.1 = (bf16[1,32,1,512]{3,2,1,0:T(2,128)(2,1)S(1)}, bf16[1,32,1,512]{3,2,1,0:T(2,128)(2,1)S(1)}, u32[]{:S(2)}, u32[]{:S(2)}) collective-permute-start(bf16[1,32,1,512]{3,2,1,0:T(2,128)(2,1)S(1)} %get-tuple-element.8), channel_id=1, source_target_pairs={{0,1},{1,2},{2,3},{3,4},{4,5},{5,6},{6,7},{7,8},{8,9},{9,10},{10,1... | collective-permute-start | bytes 98312 | tf_op jit(solution)/shard_map/ppermute | solution.py:26
  265.5 1.3 collective-permute-start.2
  266.8 3.7 %collective-permute-done.2 = bf16[1,32,1,512]{3,2,1,0:T(2,128)(2,1)S(1)} collective-permute-done((bf16[1,32,1,512]{3,2,1,0:T(2,128)(2,1)S(1)}, bf16[1,32,1,512]{3,2,1,0:T(2,128)(2,1)S(1)}, u32[]{:S(2)}, u32[]{:S(2)}) %collective-permute-start.2) | collective-permute-done | bytes 32800 | tf_op jit(solution)/shard_map/ppermute | solution.py:29
  270.5 0.5 maximum_convert_fusion
  271.1 3.2 %fusion.14 = bf16[1,32,32,512]{3,2,1,0:T(8,128)(2,1)} fusion(f32[1,32,34,512]{3,2,1,0:T(8,128)S(1)} %maximum_convert_fusion, f32[512]{0:T(512)S(1)} %bitcast.89, f32[512]{0:T(512)S(1)} %bitcast.90, f32[512]{0:T(512)S(1)} %bitcast.83, f32[512]{0:T(512)S(1)} %bitcast.84, f32[512]{0:T(512)S(1)} %bitcast.85, f32[512]{0:T(512)S(1)} %bitcast.86, ...), kind=kLoop, calls=%fused_computation.26 | loop fusion | flops 9437184 | bytes 9979904 | tf_op jit(solution)/shard_map/convert_element_type | solution.py:118
  (27 shorter events, 1.1 us)
Async XLA Ops:
  0.0 119.5 %copy-start = (bf16[512,512]{1,0:T(8,128)(2,1)S(1)}, bf16[512,512]{1,0:T(8,128)(2,1)}, u32[]{:S(2)}) copy-start(bf16[512,512]{1,0:T(8,128)(2,1)} %param.11) | copy-start | bytes 1572868
  3.2 115.0 %all-to-all-start = ((bf16[2,32,32,512]{3,2,0,1:T(8,128)(2,1)}), bf16[2,32,32,512]{3,2,0,1:T(8,128)(2,1)S(1)}, u32[]{:S(2)}, u32[]{:S(2)}) async-start(bf16[2,32,32,512]{3,2,0,1:T(8,128)(2,1)} %copy.22), calls=%async_computation | async-start | bytes 4194304 | tf_op jit(solution)/shard_map/all_to_all | solution.py:88
  20.0 98.9 %copy-start.4 = (f32[512]{0:T(512)S(1)}, f32[512]{0:T(512)}, u32[]{:S(2)}) copy-start(f32[512]{0:T(512)} %param.9) | copy-start | bytes 6148
  119.5 1.3 copy-start.5
  122.1 2.7 copy-start.6
  124.5 2.9 %copy-start.8 = (f32[32,64,64]{1,2,0:T(8,128)}, f32[32,64,64]{1,2,0:T(8,128)S(1)}, u32[]{:S(2)}) copy-start(f32[32,64,64]{1,2,0:T(8,128)S(1)} %fusion.34) | copy-start | bytes 1572868
  133.8 2.8 %copy-start.7 = (bf16[512,512]{1,0:T(8,128)(2,1)S(1)}, bf16[512,512]{1,0:T(8,128)(2,1)}, u32[]{:S(2)}) copy-start(bf16[512,512]{1,0:T(8,128)(2,1)} %param.13) | copy-start | bytes 1572868
  245.8 14.0 %collective-permute-start = (bf16[1,32,32,512]{3,2,1,0:T(8,128)(2,1)}, bf16[1,32,32,512]{3,2,1,0:T(8,128)(2,1)}, u32[]{:S(2)}, u32[]{:S(2)}) collective-permute-start(bf16[1,32,32,512]{3,2,1,0:T(8,128)(2,1)} %get-tuple-element.5), channel_id=1, source_target_pairs={{0,16},{16,32},{32,48},{48,64},{64,80},{80,96},{96,112},{112,128},... | collective-permute-start | bytes 3145736 | tf_op jit(solution)/shard_map/ppermute | solution.py:18
  247.7 2.2 copy-start.1
  247.7 2.2 copy-start.2
  261.1 5.7 %copy-start.3 = (f32[3,3,512]{2,1,0:T(4,128)S(1)}, f32[3,3,512]{2,1,0:T(4,128)}, u32[]{:S(2)}) copy-start(f32[3,3,512]{2,1,0:T(4,128)} %param.15) | copy-start | bytes 55300
  262.3 4.5 %collective-permute-start.1 = (bf16[1,32,1,512]{3,2,1,0:T(2,128)(2,1)S(1)}, bf16[1,32,1,512]{3,2,1,0:T(2,128)(2,1)S(1)}, u32[]{:S(2)}, u32[]{:S(2)}) collective-permute-start(bf16[1,32,1,512]{3,2,1,0:T(2,128)(2,1)S(1)} %get-tuple-element.8), channel_id=1, source_target_pairs={{0,1},{1,2},{2,3},{3,4},{4,5},{5,6},{6,7},{7,8},{8,9},{9,10},{10,1... | collective-permute-start | bytes 98312 | tf_op jit(solution)/shard_map/ppermute | solution.py:26
  265.5 5.0 %collective-permute-start.2 = (bf16[1,32,1,512]{3,2,1,0:T(2,128)(2,1)S(1)}, bf16[1,32,1,512]{3,2,1,0:T(2,128)(2,1)S(1)}, u32[]{:S(2)}, u32[]{:S(2)}) collective-permute-start(bf16[1,32,1,512]{3,2,1,0:T(2,128)(2,1)S(1)} %get-tuple-element.9), channel_id=1, source_target_pairs={{1,0},{2,1},{3,2},{4,3},{5,4},{6,5},{7,6},{8,7},{9,8},{10,9},{11,1... | collective-permute-start | bytes 98312 | tf_op jit(solution)/shard_map/ppermute | solution.py:29
where the time goes:
time: 277 us; the launch traced here: 274 us
  waiting for transfers between devices  111 us (40%)
  blocking collectives  106 us (38%)
  starting transfers between devices  23.2 us (8%)
  matrix products  19.2 us (7%)
  local copies, waits for them, and re-layouts  8.35 us (3%)
  other arithmetic  6.43 us (2%)
    all_to_all x1, blocking collectives, local(): lax.all_to_all(mixed_rows, 'frm', split_axis=0, concat_axis=1, tiled=True)  106 us
    all_to_all x1, waiting for transfers between devices, local(): lax.all_to_all(video, 'frm', split_axis=1, concat_axis=0, tiled=True)  98.3 us
    all_to_all x1, starting transfers between devices, local(): lax.all_to_all(video, 'frm', split_axis=1, concat_axis=0, tiled=True)  16.7 us
    ppermute x1, waiting for transfers between devices, from_behind(): lax.ppermute(value, axis, [(source, source + steps) for source in range(i...  9.07 us
    dot_general x1, matrix products, attend_block(): jnp.einsum('bpqk,bkpc->bqpc', weights, values, preferred_element_type=jnp...  6.38 us
  transfers between devices with their start and end apart: 4, of which 3 were waited for; matrix products, arithmetic and copies ran while one was open for 1% of the time, Pallas kernels for 0%

commit v1 on v0

--- a/solution.py
+++ b/solution.py
@@ -10,12 +10,6 @@
 
 
 epsilon = 1e-06
-
-
-def from_behind(value, axis, steps):
-    count = lax.axis_size(axis)
-    initial, last = (max(0, -steps), min(count, count - steps))
-    return lax.ppermute(value, axis, [(source, source + steps) for source in range(initial, last)])
 
 
 def padded_2(block, sides, width):
@@ -92,17 +86,11 @@
         w_value,
         w_out,
     )
-    returned = lax.all_to_all(mixed_rows, "frm", split_axis=0, concat_axis=1, tiled=True)
-    prior_frame = from_behind(returned[-1:], "frm", 1)
-    even_frames = returned[0::2]
-    odd_frames = returned[1::2]
-    prior_frames = jnp.concatenate([prior_frame, odd_frames[:-1]], axis=0)
-    first_index = lax.axis_index("frm") * returned.shape[0] + 2 * jnp.arange(
-        even_frames.shape[0], dtype=jnp.int32
-    )
-    starts = first_index % FRAMES == 0
-    prior_frames = jnp.where(starts[:, None, None, None], even_frames, prior_frames)
-    activated = time_conv(prior_frames, even_frames, odd_frames, w_time)
+    even_frames = mixed_rows[0::2]
+    odd_frames = mixed_rows[1::2]
+    prior_frames = jnp.concatenate([mixed_rows[:1], odd_frames[:-1]], axis=0)
+    mixed_time = time_conv(prior_frames, even_frames, odd_frames, w_time)
+    activated = lax.all_to_all(mixed_time, "frm", split_axis=0, concat_axis=1, tiled=True)
     rimmed = padded_2(activated, (("col", 2),), 1)
     rows = activated.shape[1]
     cols = activated.shape[2]

time: 277 us -> 218 us (0.79)
  blocking collectives: 106 us -> 60.9 us
  waiting for transfers between devices: 111 us -> 102 us
    all_to_all x1, blocking collectives: 106 us -> 60.9 us  [local(): lax.all_to_all(mixed_time, 'frm', split_axis=0, concat_axis=1, tiled=True)]
    ppermute x1 -> x0, waiting for transfers between devices: 9.07 us -> none  [from_behind(): lax.ppermute(value, axis, [(source, source + steps) for source in range(i...]
  transfers between devices with their start and end apart: 4 -> 3, of which waited for: 3 -> 2; matrix products, arithmetic and copies ran while one was open for 1% -> 0% of each run, Pallas kernels for 0% -> 0%
where the time goes in v1:
time: 218 us; the launch traced here: 215 us
  waiting for transfers between devices  102 us (47%)
  blocking collectives  60.9 us (28%)
  starting transfers between devices  21.2 us (10%)
  matrix products  17.8 us (8%)
  local copies, waits for them, and re-layouts  7.86 us (4%)
  other arithmetic  5.2 us (2%)
    all_to_all x1, waiting for transfers between devices, local(): lax.all_to_all(video, 'frm', split_axis=1, concat_axis=0, tiled=True)  98.3 us
    all_to_all x1, blocking collectives, local(): lax.all_to_all(mixed_time, 'frm', split_axis=0, concat_axis=1, tiled=True)  60.9 us
    all_to_all x1, starting transfers between devices, local(): lax.all_to_all(video, 'frm', split_axis=1, concat_axis=0, tiled=True)  16.7 us
    dot_general x1, matrix products, attend_block(): jnp.einsum('bpqk,bkpc->bqpc', weights, values, preferred_element_type=jnp...  6.39 us
    unnamed x17, local copies, waits for them, and re-layouts  4.5 us
  transfers between devices with their start and end apart: 3, of which 2 were waited for; matrix products, arithmetic and copies ran while one was open for 0% of the time, Pallas kernels for 0%

profile of v1, /device:TPU:1, one launch (start us, length us, event | category | flops | bytes accessed | tf_op | source)
XLA Modules:
  0.0 215.2 jit_solution(7165597653071314933)
XLA Ops:
  0.0 3.2 %copy.22 = bf16[2,32,32,512]{3,2,0,1:T(8,128)(2,1)} copy(bf16[2,32,32,512]{3,2,1,0:T(8,128)(2,1)} %param.8) | data formatting | bytes 4194304 | tf_op args[0]
  3.2 16.7 %all-to-all-start = ((bf16[2,32,32,512]{3,2,0,1:T(8,128)(2,1)}), bf16[2,32,32,512]{3,2,0,1:T(8,128)(2,1)S(1)}, u32[]{:S(2)}, u32[]{:S(2)}) async-start(bf16[2,32,32,512]{3,2,0,1:T(8,128)(2,1)} %copy.22), calls=%async_computation | async-start | bytes 4194304 | tf_op jit(solution)/shard_map/all_to_all | solution.py:82
  20.0 98.3 %all-to-all-done = bf16[2,32,32,512]{3,2,0,1:T(8,128)(2,1)S(1)} async-done(((bf16[2,32,32,512]{3,2,0,1:T(8,128)(2,1)}), bf16[2,32,32,512]{3,2,0,1:T(8,128)(2,1)S(1)}, u32[]{:S(2)}, u32[]{:S(2)}) %all-to-all-start) | async-done | bytes 2097184 | tf_op jit(solution)/shard_map/all_to_all | solution.py:82
  118.3 0.5 fusion.1
  118.9 0.5 fusion.3
  119.5 1.3 convolution_convert_fusion.1
  120.8 1.3 convolution_convert_fusion
  122.1 2.4 %fusion.34 = f32[32,64,64]{1,2,0:T(8,128)S(1)} fusion(bf16[64,32,512]{2,1,0:T(8,128)(2,1)S(1)} %bitcast.85, bf16[64,32,512]{2,1,0:T(8,128)(2,1)S(1)} %bitcast.84, pred[64,64]{0,1:T(8,128)(4,1)S(1)} %iota_compare_fusion), kind=kOutput, calls=%fused_computation.46 | convolution fusion | flops 134479872 | bytes 4722688 | tf_op jit(solution)/shard_map/bqpc,bkpc->bpqk/dot_general | solution.py:52
  124.5 0.3 fusion.55
  124.8 2.6 %convolution_convert_fusion.2 = bf16[2048,512]{1,0:T(8,128)(2,1)} fusion(bf16[2048,512]{1,0:T(8,128)(2,1)S(1)} %fusion.3, bf16[512,512]{1,0:T(8,128)(2,1)S(1)} %copy-done.5), kind=kOutput, calls=%fused_computation.10 | convolution fusion | flops 1074790400 | bytes 4718592 | tf_op jit(solution)/shard_map/dot_general | solution.py:48
  127.4 6.4 %convert_bitcast_fusion = bf16[1,64,32,512]{3,1,2,0:T(8,128)(2,1)} fusion(bf16[64,32,512]{2,1,0:T(8,128)(2,1)} %bitcast.83, f32[32,64]{1,0:T(8,128)S(1)} %fusion.55, f32[32,64,64]{1,2,0:T(8,128)} %copy-done.7), kind=kOutput, calls=%fused_computation.41 | convolution fusion | flops 135661632 | bytes 4726784 | tf_op jit(solution)/shard_map/bpqk,bkpc->bqpc/dot_general | solution.py:59
  133.8 2.8 %copy.29 = bf16[1,64,32,512]{3,2,1,0:T(8,128)(2,1)S(1)} copy(bf16[1,64,32,512]{3,1,2,0:T(8,128)(2,1)} %convert_bitcast_fusion) | data formatting | bytes 4194304 | tf_op jit(solution)/shard_map/convert_element_type | solution.py:61
  136.6 1.2 fusion.4
  137.9 0.2 fusion.52
  138.3 1.2 copy-done.1
  139.5 0.8 fusion.42
  140.4 0.7 fusion.40
  141.1 1.0 multiply_convert_fusion
  142.1 60.9 %all_to_all.21 = bf16[32,1,32,512]{3,2,1,0:T(8,128)(2,1)S(1)} all-to-all(bf16[32,1,32,512]{3,2,1,0:T(8,128)(2,1)S(1)} %bitcast.73), channel_id=1, replica_groups=mesh['frm'=32,'col'=16] {'frm'}, dimensions={0} | all-to-all | bytes 2097152 | tf_op jit(solution)/shard_map/all_to_all | solution.py:93
  203.1 3.2 %collective-permute-start = (bf16[1,32,1,512]{3,2,1,0:T(2,128)(2,1)S(1)}, bf16[1,32,1,512]{3,2,1,0:T(2,128)(2,1)S(1)}, u32[]{:S(2)}, u32[]{:S(2)}) collective-permute-start(bf16[1,32,1,512]{3,2,1,0:T(2,128)(2,1)S(1)} %get-tuple-element.7), channel_id=1, source_target_pairs={{0,1},{1,2},{2,3},{3,4},{4,5},{5,6},{6,7},{7,8},{8,9},{9,10},{10,1... | collective-permute-start | bytes 98312 | tf_op jit(solution)/shard_map/ppermute | solution.py:20
  206.4 1.3 collective-permute-start.1
  207.7 3.7 %collective-permute-done.1 = bf16[1,32,1,512]{3,2,1,0:T(2,128)(2,1)S(1)} collective-permute-done((bf16[1,32,1,512]{3,2,1,0:T(2,128)(2,1)S(1)}, bf16[1,32,1,512]{3,2,1,0:T(2,128)(2,1)S(1)}, u32[]{:S(2)}, u32[]{:S(2)}) %collective-permute-start.1) | collective-permute-done | bytes 32800 | tf_op jit(solution)/shard_map/ppermute | solution.py:23
  211.4 0.5 maximum_convert_fusion
  211.9 3.3 %fusion.14 = bf16[1,32,32,512]{3,2,1,0:T(8,128)(2,1)} fusion(f32[1,32,34,512]{3,2,1,0:T(8,128)S(1)} %maximum_convert_fusion, f32[512]{0:T(512)S(1)} %bitcast.81, f32[512]{0:T(512)S(1)} %bitcast.82, f32[512]{0:T(512)S(1)} %bitcast.75, f32[512]{0:T(512)S(1)} %bitcast.76, f32[512]{0:T(512)S(1)} %bitcast.77, f32[512]{0:T(512)S(1)} %bitcast.78, ...), kind=kLoop, calls=%fused_computation.26 | loop fusion | flops 9437184 | bytes 9979904 | tf_op jit(solution)/shard_map/convert_element_type | solution.py:106
  (25 shorter events, 0.5 us)
Async XLA Ops:
  0.0 119.5 %copy-start = (bf16[512,512]{1,0:T(8,128)(2,1)S(1)}, bf16[512,512]{1,0:T(8,128)(2,1)}, u32[]{:S(2)}) copy-start(bf16[512,512]{1,0:T(8,128)(2,1)} %param.10) | copy-start | bytes 1572868
  3.2 115.0 %all-to-all-start = ((bf16[2,32,32,512]{3,2,0,1:T(8,128)(2,1)}), bf16[2,32,32,512]{3,2,0,1:T(8,128)(2,1)S(1)}, u32[]{:S(2)}, u32[]{:S(2)}) async-start(bf16[2,32,32,512]{3,2,0,1:T(8,128)(2,1)} %copy.22), calls=%async_computation | async-start | bytes 4194304 | tf_op jit(solution)/shard_map/all_to_all | solution.py:82
  20.0 98.9 %copy-start.3 = (f32[512]{0:T(512)S(1)}, f32[512]{0:T(512)}, u32[]{:S(2)}) copy-start(f32[512]{0:T(512)} %param.9) | copy-start | bytes 6148
  119.5 1.3 copy-start.4
  122.1 2.7 %copy-start.5 = (bf16[512,512]{1,0:T(8,128)(2,1)S(1)}, bf16[512,512]{1,0:T(8,128)(2,1)}, u32[]{:S(2)}) copy-start(bf16[512,512]{1,0:T(8,128)(2,1)} %param.12) | copy-start | bytes 1572868
  124.5 2.9 %copy-start.7 = (f32[32,64,64]{1,2,0:T(8,128)}, f32[32,64,64]{1,2,0:T(8,128)S(1)}, u32[]{:S(2)}) copy-start(f32[32,64,64]{1,2,0:T(8,128)S(1)} %fusion.34) | copy-start | bytes 1572868
  133.8 2.8 %copy-start.6 = (bf16[512,512]{1,0:T(8,128)(2,1)S(1)}, bf16[512,512]{1,0:T(8,128)(2,1)}, u32[]{:S(2)}) copy-start(bf16[512,512]{1,0:T(8,128)(2,1)} %param.13) | copy-start | bytes 1572868
  138.1 1.4 copy-start.1
  142.1 65.5 %copy-start.2 = (f32[3,3,512]{2,1,0:T(4,128)S(1)}, f32[3,3,512]{2,1,0:T(4,128)}, u32[]{:S(2)}) copy-start(f32[3,3,512]{2,1,0:T(4,128)} %param.15) | copy-start | bytes 55300
  203.1 4.5 %collective-permute-start = (bf16[1,32,1,512]{3,2,1,0:T(2,128)(2,1)S(1)}, bf16[1,32,1,512]{3,2,1,0:T(2,128)(2,1)S(1)}, u32[]{:S(2)}, u32[]{:S(2)}) collective-permute-start(bf16[1,32,1,512]{3,2,1,0:T(2,128)(2,1)S(1)} %get-tuple-element.7), channel_id=1, source_target_pairs={{0,1},{1,2},{2,3},{3,4},{4,5},{5,6},{6,7},{7,8},{8,9},{9,10},{10,1... | collective-permute-start | bytes 98312 | tf_op jit(solution)/shard_map/ppermute | solution.py:20
  206.4 5.0 %collective-permute-start.1 = (bf16[1,32,1,512]{3,2,1,0:T(2,128)(2,1)S(1)}, bf16[1,32,1,512]{3,2,1,0:T(2,128)(2,1)S(1)}, u32[]{:S(2)}, u32[]{:S(2)}) collective-permute-start(bf16[1,32,1,512]{3,2,1,0:T(2,128)(2,1)S(1)} %get-tuple-element.8), channel_id=1, source_target_pairs={{1,0},{2,1},{3,2},{4,3},{5,4},{6,5},{7,6},{8,7},{9,8},{10,9},{11,1... | collective-permute-start | bytes 98312 | tf_op jit(solution)/shard_map/ppermute | solution.py:23

commit v2 on v1

v2 whole, which is shorter than its diff:
```python
import functools
import math

import jax
import jax.numpy as jnp
from jax import lax
from jax.experimental import pallas as pl
from jax.experimental.pallas import tpu as pltpu
from jax.sharding import PartitionSpec as P

MESH = pl.DeviceIdType.MESH
EPSILON = 1e-06
BLOCK = 8


def attend(slab, gain, w_query, w_key, w_value, w_out):
    rows, channels = slab.shape
    scale = lax.rsqrt(jnp.mean(slab * slab, axis=-1, keepdims=True) + EPSILON)
    normed = (slab * scale * gain).astype(jnp.bfloat16)
    queries = jnp.dot(normed, w_query, preferred_element_type=jnp.float32).astype(jnp.bfloat16)
    key_proj = jnp.dot(normed, w_key, preferred_element_type=jnp.float32).astype(jnp.bfloat16)
    values = jnp.dot(normed, w_value, preferred_element_type=jnp.float32).astype(jnp.bfloat16)
    scores = lax.dot_general(
        queries, key_proj, (((1,), (1,)), ((), ())), preferred_element_type=jnp.float32
    ) * (1.0 / math.sqrt(channels))
    ahead = lax.broadcasted_iota(jnp.int32, (rows, rows), 0) - lax.broadcasted_iota(
        jnp.int32, (rows, rows), 1
    )
    seen = (ahead >= 0) & ((ahead & (BLOCK - 1)) == 0)
    scores = jnp.where(seen, scores, -1e30)
    raised = jnp.exp(scores - jnp.max(scores, axis=-1, keepdims=True))
    weights = (raised / jnp.sum(raised, axis=-1, keepdims=True)).astype(jnp.bfloat16)
    attended = jnp.dot(weights, values, preferred_element_type=jnp.float32).astype(jnp.bfloat16)
    return slab + jnp.dot(attended, w_out, preferred_element_type=jnp.float32)


def time_conv(mixed, w_time):
    rows, channels = mixed.shape
    pairs = mixed.reshape(rows // (2 * BLOCK), 2 * BLOCK, channels)
    even = pairs[:, :BLOCK].reshape(rows // 2, channels)
    odd = pairs[:, BLOCK:].reshape(rows // 2, channels)
    prior = jnp.concatenate([even[:BLOCK], odd[:-BLOCK]], axis=0)
    summed = jnp.dot(prior.astype(jnp.bfloat16), w_time[0], preferred_element_type=jnp.float32)
    summed += jnp.dot(even.astype(jnp.bfloat16), w_time[1], preferred_element_type=jnp.float32)
    summed += jnp.dot(odd.astype(jnp.bfloat16), w_time[2], preferred_element_type=jnp.float32)
    return summed / (1.0 + jnp.exp(-summed))


def kernel(
    n,
    n_col,
    video,
    gain,
    w_query,
    w_key,
    w_value,
    w_out,
    w_time,
    w_depth,
    out,
    slabs,
    acts,
    frame,
    low_rim,
    high_rim,
    wq,
    wk,
    wv,
    wo,
    wt,
    taps,
    weight_sem,
    own_sem,
    slab_send,
    slab_recv,
    own_act_sem,
    act_send,
    act_recv,
    rim_send,
    rim_recv,
):
    me = lax.axis_index("frm")
    col = lax.axis_index("col")
    chunks, frames, _, channels = slabs.shape
    chips = n // 2
    rows = n
    chip, core = me // 2, me % 2

    weights = [
        pltpu.make_async_copy(source, target, weight_sem.at[i])
        for i, (source, target) in enumerate(
            ((w_query, wq), (w_key, wk), (w_value, wv), (w_out, wo), (w_time, wt))
        )
    ]
    for copy in weights:
        copy.start()

    barrier = pltpu.get_barrier_semaphore()

    @pl.loop(1, n)
    def _(step):
        pl.semaphore_signal(
            barrier, inc=1, device_id={"frm": (me + step) % n}, device_id_type=MESH
        )

    right, left = (col + 1) % n_col, (col + n_col - 1) % n_col
    for neighbour in (left, right):
        pl.semaphore_signal(barrier, inc=1, device_id={"col": neighbour}, device_id_type=MESH)

    for edge in (0, rows + 1):
        frame[:, edge] = jnp.zeros((chunks, BLOCK, channels), frame.dtype)
    for tap in range(9):
        taps[tap] = jnp.broadcast_to(w_depth[pl.ds(tap, 1), :], (BLOCK, channels))

    def columns(step):
        return pl.ds(pl.multiple_of((step * (chunks - 1)) % chunks * BLOCK, BLOCK), BLOCK)

    def own_slab(step):
        return pltpu.make_async_copy(
            video.at[:, me, columns(step)], slabs.at[step, pl.ds(2 * me, 2)], own_sem.at[step]
        )

    for step in range(chunks):
        own_slab(step).start()

    pl.semaphore_wait(barrier, n - 1 + 2)

    def partner(turn):
        hop, other = (turn + 1) // 2, (turn + 1) % 2
        away = (hop + 1) // 2
        signed = away * (2 * (hop % 2) - 1)
        return (chip + signed + chips) % chips * 2 + (core + other) % 2

    def send_slab(step, turn):
        to = partner(turn)
        pltpu.make_async_remote_copy(
            src_ref=video.at[:, to, columns(step)],
            dst_ref=slabs.at[step, pl.ds(2 * me, 2)],
            send_sem=slab_send,
            recv_sem=slab_recv.at[step],
            device_id={"frm": to},
            device_id_type=MESH,
        ).start()

    @pl.loop(0, chunks)
    def _(step):
        @pl.loop(0, n - 1)
        def _(turn):
            send_slab(step, turn)

    for copy in weights:
        copy.wait()

    @pl.loop(0, chunks)
    def _(step):
        own_slab(step).wait()
        arrived = slabs.at[step, pl.ds(0, frames - 2)]
        pltpu.make_async_copy(arrived, arrived, slab_recv.at[step]).wait()
        slab = slabs[step].astype(jnp.float32).reshape(frames * BLOCK, channels)
        mixed = attend(slab, gain[...], wq[...], wk[...], wv[...], wo[...])
        activated = time_conv(mixed, wt)
        acts[step] = activated.reshape(rows, BLOCK, channels).astype(acts.dtype)
        pltpu.make_async_copy(
            acts.at[step, me], frame.at[step, me + 1], own_act_sem.at[step]
        ).start()

        @pl.loop(0, n - 1)
        def _(turn):
            to = partner(n - 2 - turn)
            pltpu.make_async_remote_copy(
                src_ref=acts.at[step, to],
                dst_ref=frame.at[step, me + 1],
                send_sem=act_send,
                recv_sem=act_recv.at[step],
                device_id={"frm": to},
                device_id_type=MESH,
            ).start()

    def wait_frame(step):
        pltpu.make_async_copy(
            acts.at[step, me], frame.at[step, me + 1], own_act_sem.at[step]
        ).wait()
        arrived = frame.at[step, pl.ds(0, rows - 1)]
        pltpu.make_async_copy(arrived, arrived, act_recv.at[step]).wait()

    wait_frame(0)
    to_left = pltpu.make_async_remote_copy(
        src_ref=frame.at[0],
        dst_ref=high_rim,
        send_sem=rim_send.at[0],
        recv_sem=rim_recv.at[0],
        device_id={"col": left},
        device_id_type=MESH,
    )
    to_left.start()
    wait_frame(1)
    to_right = pltpu.make_async_remote_copy(
        src_ref=frame.at[1],
        dst_ref=low_rim,
        send_sem=rim_send.at[1],
        recv_sem=rim_recv.at[1],
        device_id={"col": right},
        device_id_type=MESH,
    )
    to_right.start()
    for step in range(2, chunks):
        wait_frame(step)
    to_left.wait()
    to_right.wait()

    has_left = jnp.where(col > 0, 1.0, 0.0)
    has_right = jnp.where(col < n_col - 1, 1.0, 0.0)
    width = chunks * BLOCK
    lanes = 256
    order = [(chunks - block) % chunks for block in range(chunks)]

    @pl.loop(0, rows)
    def _(row):
        for lane in range(0, channels, lanes):
            span = pl.ds(lane, lanes)
            sums = [None, None, None]
            low = high = None
            for a in range(3):
                line = jnp.concatenate(
                    [frame[chunk, row + a, :, span].astype(jnp.float32) for chunk in order], axis=0
                )
                line = line.reshape(chunks, BLOCK, lanes)
                for b in range(3):
                    term = line * taps[3 * a + b, :, span]
                    sums[b] = term if a == 0 else sums[b] + term
                below = low_rim[row + a, :, span].astype(jnp.float32) * taps[3 * a, :, span]
                above = high_rim[row + a, :, span].astype(jnp.float32) * taps[3 * a + 2, :, span]
                low = below if a == 0 else low + below
                high = above if a == 0 else high + above
            place = lax.broadcasted_iota(jnp.int32, (width, lanes), 0)
            before = pltpu.roll(sums[0].reshape(width, lanes), 1, 0)
            after = pltpu.roll(sums[2].reshape(width, lanes), width - 1, 0)
            low = jnp.where(has_left > 0.0, low[BLOCK - 1 :], 0.0)
            high = jnp.where(has_right > 0.0, high[:1], 0.0)
            before = jnp.where(place == 0, low, before)
            after = jnp.where(place == width - 1, high, after)
            total = before + sums[1].reshape(width, lanes) + after
            out[0, row, :, span] = total.astype(out.dtype)

    sent = slabs.at[:, pl.ds(0, frames - 2)]
    pltpu.make_async_copy(sent, sent, slab_send).wait()
    sent = acts.at[:, pl.ds(0, rows - 1)]
    pltpu.make_async_copy(sent, sent, act_send).wait()


def solution(mesh):
    n, n_col = mesh.shape["frm"], mesh.shape["col"]

    def local(video, norm_gain, w_query, w_key, w_value, w_out, w_time, w_depth):
        own, rows, cols, channels = video.shape
        chunks = cols // BLOCK
        any_space = pl.BlockSpec(memory_space=pl.ANY)
        vmem = pl.BlockSpec(memory_space=pltpu.VMEM)
        square = pltpu.VMEM((channels, channels), jnp.bfloat16)
        dma = pltpu.SemaphoreType.DMA
        return pl.pallas_call(
            functools.partial(kernel, n, n_col),
            out_shape=jax.ShapeDtypeStruct((1, rows, cols, channels), jnp.bfloat16),
            in_specs=[any_space, vmem] + [any_space] * 5 + [vmem],
            out_specs=vmem,
            scratch_shapes=[
                pltpu.VMEM((chunks, own * n, BLOCK, channels), jnp.bfloat16),
                pltpu.VMEM((chunks, n, BLOCK, channels), jnp.bfloat16),
                pltpu.VMEM((chunks, rows + 2, BLOCK, channels), jnp.bfloat16),
                pltpu.VMEM((rows + 2, BLOCK, channels), jnp.bfloat16),
                pltpu.VMEM((rows + 2, BLOCK, channels), jnp.bfloat16),
                square,
                square,
                square,
                square,
                pltpu.VMEM((3, channels, channels), jnp.bfloat16),
                pltpu.VMEM((9, BLOCK, channels), jnp.float32),
                dma((5,)),
                dma((chunks,)),
                dma,
                dma((chunks,)),
                dma((chunks,)),
                dma,
                dma((chunks,)),
                dma((2,)),
                dma((2,)),
            ],
            compiler_params=pltpu.CompilerParams(collective_id=0, has_side_effects=True),
        )(
            video,
            norm_gain.reshape(1, channels),
            w_query,
            w_key,
            w_value,
            w_out,
            w_time,
            w_depth.reshape(9, channels),
        )

    return jax.shard_map(
        local,
        mesh=mesh,
        in_specs=(P("frm", None, "col", None), P(), P(), P(), P(), P(), P(), P()),
        out_specs=P("frm", None, "col", None),
        check_vma=False,
    )
```

time: 218 us -> 161 us (0.74); the launches traced: 215 us -> 161 us
  Pallas kernels: 0 us -> 157 us
  waiting for transfers between devices: 102 us -> 0 us
  blocking collectives: 60.9 us -> 0 us
  starting transfers between devices: 21.2 us -> 0 us
  matrix products: 17.8 us -> 0 us
  other arithmetic: 5.2 us -> 0 us
  local copies, waits for them, and re-layouts: 7.86 us -> 3.67 us
    pallas_call x0 -> x1, Pallas kernels: none -> 157 us  [local(): pl.pallas_call(functools.partial(kernel, n, n_col), out_shape=jax.ShapeDt...]
    all_to_all x1 -> x0, waiting for transfers between devices: 98.3 us -> none  [local(): lax.all_to_all(video, 'frm', split_axis=1, concat_axis=0, tiled=True)]
    all_to_all x1 -> x0, blocking collectives: 60.9 us -> none  [local(): lax.all_to_all(mixed_time, 'frm', split_axis=0, concat_axis=1, tiled=True)]
    dot_general x9 -> x0, matrix products: 17.8 us -> none  [the longest x1 6.39 us: attend_block(): jnp.einsum('bpqk,bkpc->bqpc', weights, values, preferred_element_type=jnp...]
    all_to_all x1 -> x0, starting transfers between devices: 16.7 us -> none  [local(): lax.all_to_all(video, 'frm', split_axis=1, concat_axis=0, tiled=True)]
    ppermute x2 -> x0, starting transfers between devices: 4.5 us -> none  [the longest x1 3.2 us: padded_2(): lax.ppermute(lax.slice_in_dim(block, block.shape[dim] - width, None, axis...]
    convert_element_type x3 -> x0, other arithmetic: 4.34 us -> none  [the longest x1 3.26 us: local(): return summed.astype(jnp.bfloat16)]
    ppermute x2 -> x0, waiting for transfers between devices: 3.67 us -> none  [the longest x1 3.67 us: padded_2(): lax.ppermute(lax.slice_in_dim(block, 0, width, axis=dim), axis, backward)]
  transfers between devices with their start and end apart: 3 -> 0, of which waited for: 2 -> 0; matrix products, arithmetic and copies ran while one was open for 0% -> 0% of each run, Pallas kernels for 0% -> 0%
where the time goes in v2:
time: 161 us
  Pallas kernels  157 us (98%)
  local copies, waits for them, and re-layouts  3.67 us (2%)
    pallas_call x1, Pallas kernels, local(): pl.pallas_call(functools.partial(kernel, n, n_col), out_shape=jax.ShapeDt...  157 us

profile of v2, /device:TPU:1, one launch (start us, length us, event | category | flops | bytes accessed | tf_op | source)
XLA Modules:
  0.0 160.5 jit_solution(10970813843686761576)
XLA Ops:
  0.0 1.4 reshape.7.w_depth
  1.4 156.9 %shard_map.82 = bf16[1,32,32,512]{3,2,1,0:T(8,128)(2,1)} custom-call(bf16[2,32,32,512]{3,2,1,0:T(8,128)(2,1)} %video.1, f32[1,512]{1,0:T(1,128)} %bitcast.1, bf16[512,512]{1,0:T(8,128)(2,1)} %w_query.1, bf16[512,512]{1,0:T(8,128)(2,1)} %w_key.1, bf16[512,512]{1,0:T(8,128)(2,1)} %w_value.1, bf16[512,512]{1,0:T(8,128)(2,1)} %w_out.1, ...), custom_call_target="tpu_custom_call" | custom-call | tf_op jit(solution)/shard_map/pallas_call | solution.py:261
  158.2 2.3 %copy.10 = bf16[1,32,32,512]{3,2,1,0:T(8,128)(2,1)} copy(bf16[1,32,32,512]{3,2,1,0:T(8,128)(2,1)} %shard_map.82) | data formatting | bytes 2097152

commit v3 on v2

v3 whole, which is shorter than its diff:
```python
import functools
import math

import jax
import jax.numpy as jnp
from jax import lax
from jax.experimental import pallas as pl
from jax.experimental.pallas import tpu as pltpu
from jax.sharding import PartitionSpec as P

MESH = pl.DeviceIdType.MESH
EPSILON = 1e-06
BLOCK = 8
NEAR = 2
LANES = 128
GROUP = 4


def attend(slab, gain, w_query, w_key, w_value, w_out):
    rows, channels = slab.shape
    scale = lax.rsqrt(jnp.mean(slab * slab, axis=-1, keepdims=True) + EPSILON)
    normed = (slab * scale * gain).astype(jnp.bfloat16)
    queries = jnp.dot(normed, w_query, preferred_element_type=jnp.float32).astype(jnp.bfloat16)
    key_proj = jnp.dot(normed, w_key, preferred_element_type=jnp.float32).astype(jnp.bfloat16)
    values = jnp.dot(normed, w_value, preferred_element_type=jnp.float32).astype(jnp.bfloat16)
    scores = lax.dot_general(
        queries, key_proj, (((1,), (1,)), ((), ())), preferred_element_type=jnp.float32
    ) * (1.0 / math.sqrt(channels))
    ahead = lax.broadcasted_iota(jnp.int32, (rows, rows), 0) - lax.broadcasted_iota(
        jnp.int32, (rows, rows), 1
    )
    seen = (ahead >= 0) & ((ahead & (BLOCK - 1)) == 0)
    scores = jnp.where(seen, scores, -1e30)
    raised = jnp.exp(scores - jnp.max(scores, axis=-1, keepdims=True))
    weights = (raised / jnp.sum(raised, axis=-1, keepdims=True)).astype(jnp.bfloat16)
    attended = jnp.dot(weights, values, preferred_element_type=jnp.float32).astype(jnp.bfloat16)
    return slab + jnp.dot(attended, w_out, preferred_element_type=jnp.float32)


def time_conv(mixed, w_time):
    rows, channels = mixed.shape
    pairs = mixed.reshape(rows // (2 * BLOCK), 2 * BLOCK, channels)
    even = pairs[:, :BLOCK].reshape(rows // 2, channels)
    odd = pairs[:, BLOCK:].reshape(rows // 2, channels)
    prior = jnp.concatenate([even[:BLOCK], odd[:-BLOCK]], axis=0)
    summed = jnp.dot(prior.astype(jnp.bfloat16), w_time[0], preferred_element_type=jnp.float32)
    summed += jnp.dot(even.astype(jnp.bfloat16), w_time[1], preferred_element_type=jnp.float32)
    summed += jnp.dot(odd.astype(jnp.bfloat16), w_time[2], preferred_element_type=jnp.float32)
    return summed / (1.0 + jnp.exp(-summed))


def exchange(
    n,
    n_col,
    video,
    gain,
    w_query,
    w_key,
    w_value,
    w_out,
    w_time,
    frame,
    low_rim,
    high_rim,
    slabs,
    acts,
    wq,
    wk,
    wv,
    wo,
    wt,
    weight_sem,
    own_sem,
    slab_send,
    slab_recv,
    own_act_sem,
    act_send,
    act_recv,
    rim_send,
    rim_recv,
    right_known,
    left_known,
):
    me = lax.axis_index("frm")
    col = lax.axis_index("col")
    chunks, frames, _, channels = slabs.shape
    chips = n // 2
    rows = n
    chip, core = me // 2, me % 2
    far = chips // 2

    weights = [
        pltpu.make_async_copy(source, target, weight_sem.at[i])
        for i, (source, target) in enumerate(
            ((w_query, wq), (w_key, wk), (w_value, wv), (w_out, wo), (w_time, wt))
        )
    ]

    def device(away, other):
        return (chip + away + chips) % chips * 2 + (core + other) % 2

    barrier = pltpu.get_barrier_semaphore()
    for away in (1, -1):
        for other in (0, 1):
            pl.semaphore_signal(
                barrier, inc=1, device_id={"frm": device(away, other)}, device_id_type=MESH
            )
    pl.semaphore_signal(barrier, inc=1, device_id={"frm": device(0, 1)}, device_id_type=MESH)
    right, left = (col + 1) % n_col, (col + n_col - 1) % n_col
    for neighbour in (left, right):
        pl.semaphore_signal(barrier, inc=1, device_id={"col": neighbour}, device_id_type=MESH)

    def columns(step):
        return pl.ds(pl.multiple_of((step * (chunks - 1)) % chunks * BLOCK, BLOCK), BLOCK)

    def own_slab(step):
        return pltpu.make_async_copy(
            video.at[:, me, columns(step)], slabs.at[step, pl.ds(2 * me, 2)], own_sem.at[step]
        )

    for copy in weights:
        copy.start()
    for step in range(chunks):
        own_slab(step).start()

    pl.semaphore_wait(barrier, 7)

    def send_slab(step, to):
        pltpu.make_async_remote_copy(
            src_ref=video.at[:, to, columns(step)],
            dst_ref=slabs.at[step, pl.ds(2 * me, 2)],
            send_sem=slab_send,
            recv_sem=slab_recv.at[step],
            device_id={"frm": to},
            device_id_type=MESH,
        ).start()

    def send_slabs(first, last, away):
        @pl.loop(first, last)
        def _(step):
            for side in (1, -1) if away < far else (1,):
                for other in (0, 1):
                    send_slab(step, device(side * away, other))

    for away in range(1, far + 1):
        for side, known, reach in ((1, right_known, far), (-1, left_known, far - 1)):
            if 1 < away <= reach:
                pl.semaphore_wait(known.at[away], 1)
            if away < reach:
                pl.semaphore_signal(
                    known.at[away + 1],
                    inc=1,
                    device_id={"frm": device(-side, 0)},
                    device_id_type=MESH,
                )
        send_slabs(0, chunks if away <= NEAR else 1, away)
        if away == 1:

            @pl.loop(0, chunks)
            def _(step):
                send_slab(step, device(0, 1))

    @pl.loop(1, chunks)
    def _(step):
        @pl.loop(NEAR + 1, far)
        def _(away):
            for side in (1, -1):
                for other in (0, 1):
                    send_slab(step, device(side * away, other))

        for other in (0, 1):
            send_slab(step, device(far, other))

    for copy in weights:
        copy.wait()

    def partner(turn):
        hop, other = (turn + 1) // 2, (turn + 1) % 2
        return device((hop + 1) // 2 * (2 * (hop % 2) - 1), other)

    def own_act(step):
        return pltpu.make_async_copy(
            acts.at[step, me], frame.at[me, columns(step)], own_act_sem.at[step]
        )

    @pl.loop(0, chunks)
    def _(step):
        own_slab(step).wait()
        arrived = slabs.at[step, pl.ds(0, frames - 2)]
        pltpu.make_async_copy(arrived, arrived, slab_recv.at[step]).wait()
        slab = slabs[step].astype(jnp.float32).reshape(frames * BLOCK, channels)
        mixed = attend(slab, gain[...], wq[...], wk[...], wv[...], wo[...])
        activated = time_conv(mixed, wt)
        acts[step] = activated.reshape(rows, BLOCK, channels).astype(acts.dtype)
        own_act(step).start()

        @pl.loop(0, n - 1)
        def _(turn):
            to = partner(n - 2 - turn)
            pltpu.make_async_remote_copy(
                src_ref=acts.at[step, to],
                dst_ref=frame.at[me, columns(step)],
                send_sem=act_send,
                recv_sem=act_recv.at[step],
                device_id={"frm": to},
                device_id_type=MESH,
            ).start()

    def wait_frame(step):
        own_act(step).wait()
        arrived = frame.at[pl.ds(0, rows - 1), columns(step)]
        pltpu.make_async_copy(arrived, arrived, act_recv.at[step]).wait()

    def rim(step, target, neighbour):
        return pltpu.make_async_remote_copy(
            src_ref=frame.at[:, columns(step)],
            dst_ref=target,
            send_sem=rim_send.at[step],
            recv_sem=rim_recv.at[step],
            device_id={"col": neighbour},
            device_id_type=MESH,
        )

    to_left, to_right = rim(0, high_rim, left), rim(1, low_rim, right)
    wait_frame(0)
    to_left.start()
    wait_frame(1)
    to_right.start()
    for step in range(2, chunks):
        wait_frame(step)
    to_left.wait()
    to_right.wait()

    sent = slabs.at[:, pl.ds(0, frames - 2)]
    pltpu.make_async_copy(sent, sent, slab_send).wait()
    sent = acts.at[:, pl.ds(0, rows - 1)]
    pltpu.make_async_copy(sent, sent, act_send).wait()


def depthwise(n_col, frame, low_rim, high_rim, w_depth, out, image, low, high, result, sems, out_sems):
    col = lax.axis_index("col")
    rows, width, channels = frame.shape
    tiles = channels // LANES

    def loads(tile):
        span = pl.ds(tile * LANES, LANES)
        inside = pl.ds(1, rows)
        return [
            pltpu.make_async_copy(
                source.at[:, :, span], target.at[inside, :, span], sems.at[tile, i]
            )
            for i, (source, target) in enumerate(((frame, image), (low_rim, low), (high_rim, high)))
        ]

    def store(tile):
        span = pl.ds(tile * LANES, LANES)
        return pltpu.make_async_copy(
            result.at[:, :, span], out.at[0, :, :, span], out_sems.at[tile]
        )

    for tile in range(tiles):
        for copy in loads(tile):
            copy.start()
    for target in (image, low, high):
        for edge in (0, rows + 1):
            target[edge] = jnp.zeros(target.shape[1:], target.dtype)
    has_left, has_right = col > 0, col < n_col - 1
    place = lax.broadcasted_iota(jnp.int32, (width, LANES), 0)

    for tile in range(tiles):
        for copy in loads(tile):
            copy.wait()
        span = pl.ds(tile * LANES, LANES)
        taps = [[w_depth[a, pl.ds(b, 1), span] for b in range(3)] for a in range(3)]

        @pl.loop(0, rows // GROUP)
        def _(group):
            row = group * GROUP
            lines = [image[row + a, :, span].astype(jnp.float32) for a in range(GROUP + 2)]
            lows = [low[row + a, :, span].astype(jnp.float32) for a in range(GROUP + 2)]
            highs = [high[row + a, :, span].astype(jnp.float32) for a in range(GROUP + 2)]

            def column_sum(values, r, b):
                return values[r] * taps[0][b] + values[r + 1] * taps[1][b] + values[r + 2] * taps[2][b]

            for r in range(GROUP):
                before = pltpu.roll(column_sum(lines, r, 0), 1, 0)
                after = pltpu.roll(column_sum(lines, r, 2), width - 1, 0)
                first = jnp.where(has_left, column_sum(lows, r, 0)[BLOCK - 1 :], 0.0)
                last = jnp.where(has_right, column_sum(highs, r, 2)[:1], 0.0)
                total = jnp.where(place == 0, first, before) + column_sum(lines, r, 1)
                total += jnp.where(place == width - 1, last, after)
                result[row + r, :, span] = total.astype(result.dtype)

        store(tile).start()
    for tile in range(tiles):
        store(tile).wait()


def solution(mesh):
    n, n_col = mesh.shape["frm"], mesh.shape["col"]

    def local(video, norm_gain, w_query, w_key, w_value, w_out, w_time, w_depth):
        own, rows, cols, channels = video.shape
        chunks = cols // BLOCK
        half = n // 4
        any_space = pl.BlockSpec(memory_space=pl.ANY)
        vmem = pl.BlockSpec(memory_space=pltpu.VMEM)
        square = pltpu.VMEM((channels, channels), jnp.bfloat16)
        dma = pltpu.SemaphoreType.DMA
        rim = jax.ShapeDtypeStruct((rows, BLOCK, channels), jnp.bfloat16)
        frame, low_rim, high_rim = pl.pallas_call(
            functools.partial(exchange, n, n_col),
            out_shape=(jax.ShapeDtypeStruct((rows, cols, channels), jnp.bfloat16), rim, rim),
            in_specs=[any_space, vmem] + [any_space] * 5,
            out_specs=[any_space] * 3,
            scratch_shapes=[
                pltpu.VMEM((chunks, own * n, BLOCK, channels), jnp.bfloat16),
                pltpu.VMEM((chunks, n, BLOCK, channels), jnp.bfloat16),
                square,
                square,
                square,
                square,
                pltpu.VMEM((3, channels, channels), jnp.bfloat16),
                dma((5,)),
                dma((chunks,)),
                dma,
                dma((chunks,)),
                dma((chunks,)),
                dma,
                dma((chunks,)),
                dma((2,)),
                dma((2,)),
                pltpu.SemaphoreType.REGULAR((half + 1,)),
                pltpu.SemaphoreType.REGULAR((half + 1,)),
            ],
            compiler_params=pltpu.CompilerParams(collective_id=0, has_side_effects=True),
        )(video, norm_gain.reshape(1, channels), w_query, w_key, w_value, w_out, w_time)
        tiles = channels // LANES
        return pl.pallas_call(
            functools.partial(depthwise, n_col),
            out_shape=jax.ShapeDtypeStruct((1, rows, cols, channels), jnp.bfloat16),
            in_specs=[any_space] * 3 + [vmem],
            out_specs=any_space,
            scratch_shapes=[
                pltpu.VMEM((rows + 2, cols, channels), jnp.bfloat16),
                pltpu.VMEM((rows + 2, BLOCK, channels), jnp.bfloat16),
                pltpu.VMEM((rows + 2, BLOCK, channels), jnp.bfloat16),
                pltpu.VMEM((rows, cols, channels), jnp.bfloat16),
                dma((tiles, 3)),
                dma((tiles,)),
            ],
        )(frame, low_rim, high_rim, w_depth)

    return jax.shard_map(
        local,
        mesh=mesh,
        in_specs=(P("frm", None, "col", None), P(), P(), P(), P(), P(), P(), P()),
        out_specs=P("frm", None, "col", None),
        check_vma=False,
    )
```

time: 161 us -> 158 us (0.981)
  local copies, waits for them, and re-layouts: 3.67 us -> 0 us
    unnamed x1 -> x0, local copies, waits for them, and re-layouts: 2.3 us -> none
    pallas_call x1 -> x2, Pallas kernels: 157 us -> 158 us  [the longest x1 153 us: local(): pl.pallas_call(functools.partial(exchange, n, n_col), out_shape=(jax.Shap...]
where the time goes in v3:
time: 158 us
  Pallas kernels  158 us (100%)
    pallas_call x1, Pallas kernels, local(): pl.pallas_call(functools.partial(exchange, n, n_col), out_shape=(jax.Shap...  153 us
    pallas_call x1, Pallas kernels, local(): pl.pallas_call(functools.partial(depthwise, n_col), out_shape=jax.ShapeDt...  4.73 us

profile of v3, /device:TPU:1, one launch (start us, length us, event | category | flops | bytes accessed | tf_op | source)
XLA Modules:
  0.0 157.6 jit_solution(6778690019522148206)
XLA Ops:
  0.0 152.8 %shard_map.82 = (bf16[32,32,512]{2,1,0:T(8,128)(2,1)}, bf16[32,8,512]{2,1,0:T(8,128)(2,1)}, bf16[32,8,512]{2,1,0:T(8,128)(2,1)}) custom-call(bf16[2,32,32,512]{3,2,1,0:T(8,128)(2,1)} %video.1, f32[1,512]{1,0:T(1,128)} %bitcast.1, bf16[512,512]{1,0:T(8,128)(2,1)} %w_query.1, bf16[512,512]{1,0:T(8,128)(2,1)} %w_key.1, bf16[512,512]{1,0:T(8,128)(2,1)} %w_value.1, ...), custom_call_target="tpu_custom_call" | custom-call | tf_op jit(solution)/shard_map/pallas_call | solution.py:312
  152.8 4.7 %shard_map.83 = bf16[1,32,32,512]{3,2,1,0:T(8,128)(2,1)} custom-call(bf16[32,32,512]{2,1,0:T(8,128)(2,1)} %get-tuple-element.8.frame, bf16[32,8,512]{2,1,0:T(8,128)(2,1)} %get-tuple-element.9.low_rim, bf16[32,8,512]{2,1,0:T(8,128)(2,1)} %get-tuple-element.10.high_rim, f32[3,3,512]{2,1,0:T(4,128)} %w_depth.1), custom_call_target="tpu_custom_call" | custom-call | tf_op jit(solution)/shard_map/pallas_call | solution.py:340

commit v4 on v3

--- a/solution.py
+++ b/solution.py
@@ -12,8 +12,8 @@
 EPSILON = 1e-06
 BLOCK = 8
 NEAR = 2
-LANES = 128
-GROUP = 4
+LANES = 256
+PIECES = 4
 
 
 def attend(slab, gain, w_query, w_key, w_value, w_out):
@@ -59,11 +59,17 @@
     w_value,
     w_out,
     w_time,
+    w_depth,
+    done,
+    middle,
+    edges,
+    slabs,
+    acts,
     frame,
     low_rim,
     high_rim,
-    slabs,
-    acts,
+    filtered,
+    partial,
     wq,
     wk,
     wv,
@@ -78,6 +84,7 @@
     act_recv,
     rim_send,
     rim_recv,
+    done_sem,
     right_known,
     left_known,
 ):
@@ -178,10 +185,27 @@
         hop, other = (turn + 1) // 2, (turn + 1) % 2
         return device((hop + 1) // 2 * (2 * (hop % 2) - 1), other)
 
+    def landing(step, row):
+        return middle.at[row] if step == chunks - 1 else frame.at[step, row + 1]
+
     def own_act(step):
-        return pltpu.make_async_copy(
-            acts.at[step, me], frame.at[me, columns(step)], own_act_sem.at[step]
-        )
+        return pltpu.make_async_copy(acts.at[step, me], landing(step, me), own_act_sem.at[step])
+
+    def send_acts(step, recv_step, target):
+        @pl.loop(0, n - 1)
+        def _(turn):
+            to = partner(n - 2 - turn)
+            pltpu.make_async_remote_copy(
+                src_ref=acts.at[step, to],
+                dst_ref=target,
+                send_sem=act_send,
+                recv_sem=act_recv.at[recv_step],
+                device_id={"frm": to},
+                device_id_type=MESH,
+            ).start()
+
+    for edge in (0, rows + 1):
+        frame[:, edge] = jnp.zeros((chunks - 1, BLOCK, channels), frame.dtype)
 
     @pl.loop(0, chunks)
     def _(step):
@@ -192,28 +216,28 @@
         mixed = attend(slab, gain[...], wq[...], wk[...], wv[...], wo[...])
         activated = time_conv(mixed, wt)
         acts[step] = activated.reshape(rows, BLOCK, channels).astype(acts.dtype)
-        own_act(step).start()
-
-        @pl.loop(0, n - 1)
-        def _(turn):
-            to = partner(n - 2 - turn)
-            pltpu.make_async_remote_copy(
-                src_ref=acts.at[step, to],
-                dst_ref=frame.at[me, columns(step)],
-                send_sem=act_send,
-                recv_sem=act_recv.at[step],
-                device_id={"frm": to},
-                device_id_type=MESH,
+
+        @pl.when(step < chunks - 1)
+        def _():
+            pltpu.make_async_copy(
+                acts.at[step, me], frame.at[step, me + 1], own_act_sem.at[step]
             ).start()
+            send_acts(step, step, frame.at[step, me + 1])
+
+        @pl.when(step == chunks - 1)
+        def _():
+            own_act(chunks - 1).start()
+            send_acts(chunks - 1, chunks - 1, middle.at[me])
 
     def wait_frame(step):
         own_act(step).wait()
-        arrived = frame.at[pl.ds(0, rows - 1), columns(step)]
+        ref = middle if step == chunks - 1 else frame.at[step]
+        arrived = ref.at[pl.ds(0, rows - 1)]
         pltpu.make_async_copy(arrived, arrived, act_recv.at[step]).wait()
 
     def rim(step, target, neighbour):
         return pltpu.make_async_remote_copy(
-            src_ref=frame.at[:, columns(step)],
+            src_ref=frame.at[step],
             dst_ref=target,
             send_sem=rim_send.at[step],
             recv_sem=rim_recv.at[step],
@@ -226,75 +250,133 @@
     to_left.start()
     wait_frame(1)
     to_right.start()
-    for step in range(2, chunks):
-        wait_frame(step)
+    wait_frame(2)
     to_left.wait()
     to_right.wait()
 
+    has_left, has_right = col > 0, col < n_col - 1
+    place = lax.broadcasted_iota(jnp.int32, (BLOCK, LANES), 0)
+
+    @pl.loop(0, rows)
+    def _(row):
+        for lane in range(0, channels, LANES):
+            span = pl.ds(lane, LANES)
+
+            def column_sum(ref, b):
+                total = None
+                for a in range(3):
+                    term = ref[row + a, :, span].astype(jnp.float32) * w_depth[a, pl.ds(b, 1), span]
+                    total = term if total is None else total + term
+                return total
+
+            first, third, fourth = frame.at[0], frame.at[2], frame.at[1]
+            first_0, first_1, first_2 = (column_sum(first, b) for b in range(3))
+            third_0, third_1, third_2 = (column_sum(third, b) for b in range(3))
+            fourth_0, fourth_1, fourth_2 = (column_sum(fourth, b) for b in range(3))
+            low = pltpu.roll(column_sum(low_rim, 0), 1, 0)
+            high = pltpu.roll(column_sum(high_rim, 2), BLOCK - 1, 0)
+            low = jnp.where(has_left, low, 0.0)
+            high = jnp.where(has_right, high, 0.0)
+
+            def before(own, previous):
+                return jnp.where(place == 0, previous, pltpu.roll(own, 1, 0))
+
+            def after(own, following):
+                return jnp.where(place == BLOCK - 1, following, pltpu.roll(own, BLOCK - 1, 0))
+
+            first_part = before(first_0, low) + first_1
+            third_part = third_1 + after(third_2, pltpu.roll(fourth_2, BLOCK - 1, 0))
+            fourth_part = before(fourth_0, pltpu.roll(third_0, 1, 0)) + fourth_1
+            filtered[0, row, :, span] = (first_part + pltpu.roll(first_2, BLOCK - 1, 0)).astype(
+                filtered.dtype
+            )
+            filtered[2, row, :, span] = (third_part + pltpu.roll(third_0, 1, 0)).astype(
+                filtered.dtype
+            )
+            filtered[1, row, :, span] = (fourth_part + after(fourth_2, high)).astype(filtered.dtype)
+            kept = jnp.where(place == 0, third_part, first_part)
+            kept = jnp.where(place == 1, pltpu.roll(first_0, 2, 0), kept)
+            kept = jnp.where(place == BLOCK - 2, pltpu.roll(third_2, BLOCK - 2, 0), kept)
+            partial[row, :, span] = kept
+
+    stores = [
+        pltpu.make_async_copy(
+            filtered.at[step], done.at[:, columns(step)], done_sem.at[step]
+        )
+        for step in range(chunks - 1)
+    ]
+    stores.append(pltpu.make_async_copy(partial, edges, done_sem.at[chunks - 1]))
+    for copy in stores:
+        copy.start()
+    for copy in stores:
+        copy.wait()
     sent = slabs.at[:, pl.ds(0, frames - 2)]
     pltpu.make_async_copy(sent, sent, slab_send).wait()
+    wait_frame(chunks - 1)
     sent = acts.at[:, pl.ds(0, rows - 1)]
     pltpu.make_async_copy(sent, sent, act_send).wait()
 
 
-def depthwise(n_col, frame, low_rim, high_rim, w_depth, out, image, low, high, result, sems, out_sems):
-    col = lax.axis_index("col")
-    rows, width, channels = frame.shape
-    tiles = channels // LANES
-
-    def loads(tile):
-        span = pl.ds(tile * LANES, LANES)
-        inside = pl.ds(1, rows)
-        return [
-            pltpu.make_async_copy(
-                source.at[:, :, span], target.at[inside, :, span], sems.at[tile, i]
-            )
-            for i, (source, target) in enumerate(((frame, image), (low_rim, low), (high_rim, high)))
-        ]
-
-    def store(tile):
-        span = pl.ds(tile * LANES, LANES)
-        return pltpu.make_async_copy(
-            result.at[:, :, span], out.at[0, :, :, span], out_sems.at[tile]
-        )
-
-    for tile in range(tiles):
-        for copy in loads(tile):
-            copy.start()
-    for target in (image, low, high):
-        for edge in (0, rows + 1):
-            target[edge] = jnp.zeros(target.shape[1:], target.dtype)
-    has_left, has_right = col > 0, col < n_col - 1
-    place = lax.broadcasted_iota(jnp.int32, (width, LANES), 0)
-
-    for tile in range(tiles):
-        for copy in loads(tile):
-            copy.wait()
-        span = pl.ds(tile * LANES, LANES)
-        taps = [[w_depth[a, pl.ds(b, 1), span] for b in range(3)] for a in range(3)]
-
-        @pl.loop(0, rows // GROUP)
-        def _(group):
-            row = group * GROUP
-            lines = [image[row + a, :, span].astype(jnp.float32) for a in range(GROUP + 2)]
-            lows = [low[row + a, :, span].astype(jnp.float32) for a in range(GROUP + 2)]
-            highs = [high[row + a, :, span].astype(jnp.float32) for a in range(GROUP + 2)]
-
-            def column_sum(values, r, b):
-                return values[r] * taps[0][b] + values[r + 1] * taps[1][b] + values[r + 2] * taps[2][b]
-
-            for r in range(GROUP):
-                before = pltpu.roll(column_sum(lines, r, 0), 1, 0)
-                after = pltpu.roll(column_sum(lines, r, 2), width - 1, 0)
-                first = jnp.where(has_left, column_sum(lows, r, 0)[BLOCK - 1 :], 0.0)
-                last = jnp.where(has_right, column_sum(highs, r, 2)[:1], 0.0)
-                total = jnp.where(place == 0, first, before) + column_sum(lines, r, 1)
-                total += jnp.where(place == width - 1, last, after)
-                result[row + r, :, span] = total.astype(result.dtype)
-
-        store(tile).start()
-    for tile in range(tiles):
-        store(tile).wait()
+def finish(done, middle, edges, w_depth, out, image, inner, partial, sems, out_sems):
+    rows, width, channels = done.shape
+    band = rows // PIECES
+
+    def load(piece, i):
+        here = pl.ds(piece * band, band)
+        if i == 0:
+            source, target = middle.at[here], inner.at[pl.ds(piece * band + 1, band)]
+        elif i == 1:
+            source, target = edges.at[here], partial.at[here]
+        else:
+            span = pl.ds(0, BLOCK) if i == 2 else pl.ds(2 * BLOCK, 2 * BLOCK)
+            source, target = done.at[here, span], image.at[here, span]
+        return pltpu.make_async_copy(source, target, sems.at[piece, i])
+
+    def store(piece):
+        here = pl.ds(piece * band, band)
+        return pltpu.make_async_copy(image.at[here], out.at[0, here], out_sems.at[piece])
+
+    for piece in range(PIECES):
+        for i in range(4):
+            load(piece, i).start()
+    for edge in (0, rows + 1):
+        inner[edge] = jnp.zeros(inner.shape[1:], inner.dtype)
+    place = lax.broadcasted_iota(jnp.int32, (BLOCK, LANES), 0)
+
+    for piece in range(PIECES):
+        for i in range(1 if piece else 0, 4):
+            load(piece, i).wait()
+        if piece + 1 < PIECES:
+            load(piece + 1, 0).wait()
+
+        @pl.loop(piece * band, (piece + 1) * band)
+        def _(row):
+            for lane in range(0, channels, LANES):
+                span = pl.ds(lane, LANES)
+                lines = [inner[row + a, :, span].astype(jnp.float32) for a in range(3)]
+                sums = []
+                for b in range(3):
+                    total = lines[0] * w_depth[0, pl.ds(b, 1), span]
+                    for a in (1, 2):
+                        total += lines[a] * w_depth[a, pl.ds(b, 1), span]
+                    sums.append(total)
+                kept = partial[row, :, span]
+                before = pltpu.roll(sums[0], 1, 0)
+                after = pltpu.roll(sums[2], BLOCK - 1, 0)
+                total = sums[1] + jnp.where(place == 0, pltpu.roll(kept, BLOCK - 1, 0), before)
+                total += jnp.where(place == BLOCK - 1, pltpu.roll(kept, 1, 0), after)
+                first, third = pl.ds(0, BLOCK), pl.ds(2 * BLOCK, BLOCK)
+                image[row, pl.ds(BLOCK, BLOCK), span] = total.astype(image.dtype)
+                value = image[row, first, span].astype(jnp.float32)
+                value = jnp.where(place == BLOCK - 1, kept + after, value)
+                image[row, first, span] = value.astype(image.dtype)
+                value = image[row, third, span].astype(jnp.float32)
+                value = jnp.where(place == 0, kept + before, value)
+                image[row, third, span] = value.astype(image.dtype)
+
+        store(piece).start()
+    for piece in range(PIECES):
+        store(piece).wait()
 
 
 def solution(mesh):
@@ -308,15 +390,24 @@
         vmem = pl.BlockSpec(memory_space=pltpu.VMEM)
         square = pltpu.VMEM((channels, channels), jnp.bfloat16)
         dma = pltpu.SemaphoreType.DMA
-        rim = jax.ShapeDtypeStruct((rows, BLOCK, channels), jnp.bfloat16)
-        frame, low_rim, high_rim = pl.pallas_call(
+        block = pltpu.VMEM((rows + 2, BLOCK, channels), jnp.bfloat16)
+        done, middle, edges = pl.pallas_call(
             functools.partial(exchange, n, n_col),
-            out_shape=(jax.ShapeDtypeStruct((rows, cols, channels), jnp.bfloat16), rim, rim),
-            in_specs=[any_space, vmem] + [any_space] * 5,
+            out_shape=(
+                jax.ShapeDtypeStruct((rows, cols, channels), jnp.bfloat16),
+                jax.ShapeDtypeStruct((rows, BLOCK, channels), jnp.bfloat16),
+                jax.ShapeDtypeStruct((rows, BLOCK, channels), jnp.float32),
+            ),
+            in_specs=[any_space, vmem] + [any_space] * 5 + [vmem],
             out_specs=[any_space] * 3,
             scratch_shapes=[
                 pltpu.VMEM((chunks, own * n, BLOCK, channels), jnp.bfloat16),
                 pltpu.VMEM((chunks, n, BLOCK, channels), jnp.bfloat16),
+                pltpu.VMEM((chunks - 1, rows + 2, BLOCK, channels), jnp.bfloat16),
+                block,
+                block,
+                pltpu.VMEM((chunks - 1, rows, BLOCK, channels), jnp.bfloat16),
+                pltpu.VMEM((rows, BLOCK, channels), jnp.float32),
                 square,
                 square,
                 square,
@@ -331,26 +422,25 @@
                 dma((chunks,)),
                 dma((2,)),
                 dma((2,)),
+                dma((chunks,)),
                 pltpu.SemaphoreType.REGULAR((half + 1,)),
                 pltpu.SemaphoreType.REGULAR((half + 1,)),
             ],
             compiler_params=pltpu.CompilerParams(collective_id=0, has_side_effects=True),
-        )(video, norm_gain.reshape(1, channels), w_query, w_key, w_value, w_out, w_time)
-        tiles = channels // LANES
+        )(video, norm_gain.reshape(1, channels), w_query, w_key, w_value, w_out, w_time, w_depth)
         return pl.pallas_call(
-            functools.partial(depthwise, n_col),
+            finish,
             out_shape=jax.ShapeDtypeStruct((1, rows, cols, channels), jnp.bfloat16),
             in_specs=[any_space] * 3 + [vmem],
             out_specs=any_space,
             scratch_shapes=[
-                pltpu.VMEM((rows + 2, cols, channels), jnp.bfloat16),
-                pltpu.VMEM((rows + 2, BLOCK, channels), jnp.bfloat16),
-                pltpu.VMEM((rows + 2, BLOCK, channels), jnp.bfloat16),
                 pltpu.VMEM((rows, cols, channels), jnp.bfloat16),
-                dma((tiles, 3)),
-                dma((tiles,)),
+                block,
+                pltpu.VMEM((rows, BLOCK, channels), jnp.float32),
+                dma((PIECES, 4)),
+                dma((PIECES,)),
             ],
-        )(frame, low_rim, high_rim, w_depth)
+        )(done, middle, edges, w_depth)
 
     return jax.shard_map(
         local,

time: 158 us -> 157 us (level)
  Pallas kernels: 158 us -> 156 us
where the time goes in v4:
time: 157 us; the launch traced here: 156 us
  Pallas kernels  156 us (99%)
    pallas_call x1, Pallas kernels, local(): pl.pallas_call(functools.partial(exchange, n, n_col), out_shape=(jax.Shap...  153 us
    pallas_call x1, Pallas kernels, local(): pl.pallas_call(finish, out_shape=jax.ShapeDtypeStruct((1, rows, cols, cha...  3.42 us

profile of v4, /device:TPU:1, one launch (start us, length us, event | category | flops | bytes accessed | tf_op | source)
XLA Modules:
  0.0 156.3 jit_solution(14190225278932253076)
XLA Ops:
  0.0 152.9 %shard_map.82 = (bf16[32,32,512]{2,1,0:T(8,128)(2,1)}, bf16[32,8,512]{2,1,0:T(8,128)(2,1)}, f32[32,8,512]{2,1,0:T(8,128)}) custom-call(bf16[2,32,32,512]{3,2,1,0:T(8,128)(2,1)} %video.1, f32[1,512]{1,0:T(1,128)} %bitcast.1, bf16[512,512]{1,0:T(8,128)(2,1)} %w_query.1, bf16[512,512]{1,0:T(8,128)(2,1)} %w_key.1, bf16[512,512]{1,0:T(8,128)(2,1)} %w_value.1, ...), custom_call_target="tpu_custom_call" | custom-call | tf_op jit(solution)/shard_map/pallas_call | solution.py:394
  152.9 3.4 %shard_map.83 = bf16[1,32,32,512]{3,2,1,0:T(8,128)(2,1)} custom-call(bf16[32,32,512]{2,1,0:T(8,128)(2,1)} %get-tuple-element.8.done, bf16[32,8,512]{2,1,0:T(8,128)(2,1)} %get-tuple-element.9.middle, f32[32,8,512]{2,1,0:T(8,128)} %get-tuple-element.10.edges, f32[3,3,512]{2,1,0:T(4,128)} %w_depth.3), custom_call_target="tpu_custom_call" | custom-call | tf_op jit(solution)/shard_map/pallas_call | solution.py:431

commit v5 on v4

--- a/solution.py
+++ b/solution.py
@@ -53,13 +53,13 @@
     n,
     n_col,
     video,
-    gain,
+    gain_in,
     w_query,
     w_key,
     w_value,
     w_out,
     w_time,
-    w_depth,
+    w_depth_in,
     done,
     middle,
     edges,
@@ -75,6 +75,8 @@
     wv,
     wo,
     wt,
+    gain,
+    w_depth,
     weight_sem,
     own_sem,
     slab_send,
@@ -99,7 +101,15 @@
     weights = [
         pltpu.make_async_copy(source, target, weight_sem.at[i])
         for i, (source, target) in enumerate(
-            ((w_query, wq), (w_key, wk), (w_value, wv), (w_out, wo), (w_time, wt))
+            (
+                (w_query, wq),
+                (w_key, wk),
+                (w_value, wv),
+                (w_out, wo),
+                (w_time, wt),
+                (gain_in, gain),
+                (w_depth_in, w_depth),
+            )
         )
     ]
 
@@ -317,7 +327,9 @@
     pltpu.make_async_copy(sent, sent, act_send).wait()
 
 
-def finish(done, middle, edges, w_depth, out, image, inner, partial, sems, out_sems):
+def finish(
+    done, middle, edges, w_depth_in, out, image, inner, partial, w_depth, sems, out_sems, taps_sem
+):
     rows, width, channels = done.shape
     band = rows // PIECES
 
@@ -339,10 +351,14 @@
     for piece in range(PIECES):
         for i in range(4):
             load(piece, i).start()
+        if piece == 0:
+            taps = pltpu.make_async_copy(w_depth_in, w_depth, taps_sem)
+            taps.start()
     for edge in (0, rows + 1):
         inner[edge] = jnp.zeros(inner.shape[1:], inner.dtype)
     place = lax.broadcasted_iota(jnp.int32, (BLOCK, LANES), 0)
 
+    taps.wait()
     for piece in range(PIECES):
         for i in range(1 if piece else 0, 4):
             load(piece, i).wait()
@@ -387,7 +403,6 @@
         chunks = cols // BLOCK
         half = n // 4
         any_space = pl.BlockSpec(memory_space=pl.ANY)
-        vmem = pl.BlockSpec(memory_space=pltpu.VMEM)
         square = pltpu.VMEM((channels, channels), jnp.bfloat16)
         dma = pltpu.SemaphoreType.DMA
         block = pltpu.VMEM((rows + 2, BLOCK, channels), jnp.bfloat16)
@@ -398,7 +413,7 @@
                 jax.ShapeDtypeStruct((rows, BLOCK, channels), jnp.bfloat16),
                 jax.ShapeDtypeStruct((rows, BLOCK, channels), jnp.float32),
             ),
-            in_specs=[any_space, vmem] + [any_space] * 5 + [vmem],
+            in_specs=[any_space] * 8,
             out_specs=[any_space] * 3,
             scratch_shapes=[
                 pltpu.VMEM((chunks, own * n, BLOCK, channels), jnp.bfloat16),
@@ -413,7 +428,9 @@
                 square,
                 square,
                 pltpu.VMEM((3, channels, channels), jnp.bfloat16),
-                dma((5,)),
+                pltpu.VMEM((1, channels), jnp.float32),
+                pltpu.VMEM(w_depth.shape, jnp.float32),
+                dma((7,)),
                 dma((chunks,)),
                 dma,
                 dma((chunks,)),
@@ -431,14 +448,16 @@
         return pl.pallas_call(
             finish,
             out_shape=jax.ShapeDtypeStruct((1, rows, cols, channels), jnp.bfloat16),
-            in_specs=[any_space] * 3 + [vmem],
+            in_specs=[any_space] * 4,
             out_specs=any_space,
             scratch_shapes=[
                 pltpu.VMEM((rows, cols, channels), jnp.bfloat16),
                 block,
                 pltpu.VMEM((rows, BLOCK, channels), jnp.float32),
+                pltpu.VMEM(w_depth.shape, jnp.float32),
                 dma((PIECES, 4)),
                 dma((PIECES,)),
+                dma,
             ],
         )(done, middle, edges, w_depth)
 

time: 157 us -> 155 us (0.987)
  no operation moved by 1% of the time
where the time goes in v5:
time: 155 us
  Pallas kernels  155 us (100%)
    pallas_call x1, Pallas kernels, local(): pl.pallas_call(functools.partial(exchange, n, n_col), out_shape=(jax.Shap...  152 us

profile of v5, /device:TPU:1, one launch (start us, length us, event | category | flops | bytes accessed | tf_op | source)
XLA Modules:
  0.0 155.2 jit_solution(18027782757197687849)
XLA Ops:
  0.0 152.3 %shard_map.82 = (bf16[32,32,512]{2,1,0:T(8,128)(2,1)}, bf16[32,8,512]{2,1,0:T(8,128)(2,1)}, f32[32,8,512]{2,1,0:T(8,128)}) custom-call(bf16[2,32,32,512]{3,2,1,0:T(8,128)(2,1)} %video.1, f32[1,512]{1,0:T(1,128)} %bitcast.1, bf16[512,512]{1,0:T(8,128)(2,1)} %w_query.1, bf16[512,512]{1,0:T(8,128)(2,1)} %w_key.1, bf16[512,512]{1,0:T(8,128)(2,1)} %w_value.1, ...), custom_call_target="tpu_custom_call" | custom-call | tf_op jit(solution)/shard_map/pallas_call | solution.py:409
  152.3 2.9 %shard_map.83 = bf16[1,32,32,512]{3,2,1,0:T(8,128)(2,1)} custom-call(bf16[32,32,512]{2,1,0:T(8,128)(2,1)} %get-tuple-element.8.done, bf16[32,8,512]{2,1,0:T(8,128)(2,1)} %get-tuple-element.9.middle, f32[32,8,512]{2,1,0:T(8,128)} %get-tuple-element.10.edges, f32[3,3,512]{2,1,0:T(4,128)} %w_depth_in.3), custom_call_target="tpu_custom_call" | custom-call | tf_op jit(solution)/shard_map/pallas_call | solution.py:448

commit v6 on v5

--- a/solution.py
+++ b/solution.py
@@ -13,7 +13,7 @@
 BLOCK = 8
 NEAR = 2
 LANES = 256
-PIECES = 4
+PIECES = 8
 
 
 def attend(slab, gain, w_query, w_key, w_value, w_out):

time: 155 us -> 156 us (level)
  no operation moved by 1% of the time
where the time goes in v6:
time: 156 us; the launch traced here: 155 us
  Pallas kernels  155 us (99%)
    pallas_call x1, Pallas kernels, local(): pl.pallas_call(functools.partial(exchange, n, n_col), out_shape=(jax.Shap...  152 us

profile of v6, /device:TPU:1, one launch (start us, length us, event | category | flops | bytes accessed | tf_op | source)
XLA Modules:
  0.0 155.4 jit_solution(1462275284711585190)
XLA Ops:
  0.0 152.3 %shard_map.82 = (bf16[32,32,512]{2,1,0:T(8,128)(2,1)}, bf16[32,8,512]{2,1,0:T(8,128)(2,1)}, f32[32,8,512]{2,1,0:T(8,128)}) custom-call(bf16[2,32,32,512]{3,2,1,0:T(8,128)(2,1)} %video.1, f32[1,512]{1,0:T(1,128)} %bitcast.1, bf16[512,512]{1,0:T(8,128)(2,1)} %w_query.1, bf16[512,512]{1,0:T(8,128)(2,1)} %w_key.1, bf16[512,512]{1,0:T(8,128)(2,1)} %w_value.1, ...), custom_call_target="tpu_custom_call" | custom-call | tf_op jit(solution)/shard_map/pallas_call | solution.py:409
  152.3 3.1 %shard_map.83 = bf16[1,32,32,512]{3,2,1,0:T(8,128)(2,1)} custom-call(bf16[32,32,512]{2,1,0:T(8,128)(2,1)} %get-tuple-element.8.done, bf16[32,8,512]{2,1,0:T(8,128)(2,1)} %get-tuple-element.9.middle, f32[32,8,512]{2,1,0:T(8,128)} %get-tuple-element.10.edges, f32[3,3,512]{2,1,0:T(4,128)} %w_depth_in.3), custom_call_target="tpu_custom_call" | custom-call | tf_op jit(solution)/shard_map/pallas_call | solution.py:448

commit v7 on v6

--- a/solution.py
+++ b/solution.py
@@ -13,7 +13,7 @@
 BLOCK = 8
 NEAR = 2
 LANES = 256
-PIECES = 8
+PIECES = 2
 
 
 def attend(slab, gain, w_query, w_key, w_value, w_out):

time: 156 us -> 155 us (level)
  no operation moved by 1% of the time
where the time goes in v7:
time: 155 us
  Pallas kernels  155 us (100%)
    pallas_call x1, Pallas kernels, local(): pl.pallas_call(functools.partial(exchange, n, n_col), out_shape=(jax.Shap...  152 us

profile of v7, /device:TPU:1, one launch (start us, length us, event | category | flops | bytes accessed | tf_op | source)
XLA Modules:
  0.0 155.1 jit_solution(2469123481602385861)
XLA Ops:
  0.0 152.3 %shard_map.82 = (bf16[32,32,512]{2,1,0:T(8,128)(2,1)}, bf16[32,8,512]{2,1,0:T(8,128)(2,1)}, f32[32,8,512]{2,1,0:T(8,128)}) custom-call(bf16[2,32,32,512]{3,2,1,0:T(8,128)(2,1)} %video.1, f32[1,512]{1,0:T(1,128)} %bitcast.1, bf16[512,512]{1,0:T(8,128)(2,1)} %w_query.1, bf16[512,512]{1,0:T(8,128)(2,1)} %w_key.1, bf16[512,512]{1,0:T(8,128)(2,1)} %w_value.1, ...), custom_call_target="tpu_custom_call" | custom-call | tf_op jit(solution)/shard_map/pallas_call | solution.py:409
  152.3 2.8 %shard_map.83 = bf16[1,32,32,512]{3,2,1,0:T(8,128)(2,1)} custom-call(bf16[32,32,512]{2,1,0:T(8,128)(2,1)} %get-tuple-element.8.done, bf16[32,8,512]{2,1,0:T(8,128)(2,1)} %get-tuple-element.9.middle, f32[32,8,512]{2,1,0:T(8,128)} %get-tuple-element.10.edges, f32[3,3,512]{2,1,0:T(4,128)} %w_depth_in.3), custom_call_target="tpu_custom_call" | custom-call | tf_op jit(solution)/shard_map/pallas_call | solution.py:448
